TPU v7x, 32 devices: a whole 2x2x4 slice. The times are simulated.
32 devices in a mesh: mesh: 8 (over z, y), mode: 4 (over x, core).
Axes of the slice: x: 2, y: 2, z: 4, core: 2. Of those that a mesh axis runs over, the one named last changes fastest.
Arguments:
- field: float32 [256, 131072], P('mode', 'mesh'), may hold values from -6 to 6
- right_side: float32 [256, 131072], P('mode', 'mesh'), may hold values from -6 to 6
- coefficient: float32 [2, 131072], P(None, 'mesh'), may hold values from 0.3 to 3
- precond: float32 [131072], P('mesh'), may hold values from 0.1 to 1
- blocks: bfloat16 [2, 7, 256, 256], replicated, may hold values from -0.125 to 0.125
- couplings: int32 [512, 7], P('mesh'), may hold values from 0 to 1, as said below
- chaos_values: bfloat16 [48, 16, 16], replicated, may hold values from -0.875 to 0.875
- chaos_index: int32 [48, 2], replicated, may hold values from 0 to 15, as said below
Outputs:
- updated: float32 [256, 131072], P('mode', 'mesh')
- residual: float32 [256, 131072], P('mode', 'mesh')
Inputs may be any that keep to these rules, and one draw needn't show every extreme that they name: couplings[i, c] links block i to block i + c - 3; it is 1 for c = 3 and wherever block i + c - 3 lies in another slab of 16384 unknowns. `chaos_index`: rows 3 r to 3 r + 2 hold row block r, with column blocks r and two other distinct blocks.
All inputs are finite; a program needn't handle non-finite values.
Results may differ from a plain program's by a relative error of at most 0.0032.
Values may be sent and summed in bfloat16 or wider, within the bound.
A program may use at most 128 MiB of HBM per device.

v0:
```python
import functools

import jax
import jax.numpy as jnp
from jax import lax
from jax.experimental import pallas as pl
from jax.experimental.pallas import tpu as pltpu
from jax.sharding import PartitionSpec as P

MESH = pl.DeviceIdType.MESH
REACH = 3


def kernel(
    modes, slabs, group,
    field, right, coefficient, blocks, couplings, chaos_values, chaos_index,
    fbuf, rbuf,
    low, weights, coef, gathered, matrix, hits,
    field_sem, right_sem, weight_sem, coef_sem,
    halo_send, halo_recv, near_send, far_send, forward_send, recv,
):
    rows, width = field.shape
    size = blocks.shape[-1]
    count = width // size
    groups = count // group
    span = group * size
    taps = 2 * REACH + 1
    pairs = modes // 2
    me = lax.axis_index("mode")
    slab = lax.axis_index("mesh")
    sibling = me + 1 - 2 * lax.rem(me, 2)
    peers = [lax.rem(me + 2 * j, modes) for j in range(1, pairs)]
    has_left = slab > 0
    has_right = slab < slabs - 1

    def columns(g):
        return pl.ds(pl.multiple_of(g * span, span), span)

    def field_copy(g):
        return pltpu.make_async_copy(field.at[:, columns(g)], fbuf.at[:, columns(g)], field_sem.at[g])

    def right_copy(g):
        return pltpu.make_async_copy(right.at[:, columns(g)], rbuf.at[:, columns(g)], right_sem.at[g])

    def weight_copy(k):
        return pltpu.make_async_copy(blocks.at[k], weights.at[k], weight_sem.at[k])

    field_copy(0).start()
    field_copy(groups - 1).start()
    weight_copy(1).start()
    coef_copy = pltpu.make_async_copy(coefficient, coef, coef_sem)
    coef_copy.start()

    @pl.loop(1, groups - 1)
    def _(g):
        field_copy(g).start()

    weight_copy(0).start()

    @pl.loop(0, groups)
    def _(g):
        right_copy(g).start()

    barrier = pltpu.get_barrier_semaphore()
    for other in [sibling] + peers:
        pl.semaphore_signal(barrier, inc=1, device_id={"mode": other}, device_id_type=MESH)

    @pl.when(has_left)
    def _():
        pl.semaphore_signal(barrier, inc=1, device_id={"mesh": slab - 1}, device_id_type=MESH)

    @pl.when(has_right)
    def _():
        pl.semaphore_signal(barrier, inc=1, device_id={"mesh": slab + 1}, device_id_type=MESH)

    def lower(g):
        for b in range(group):
            at = g * group + b
            cols = pl.ds(pl.multiple_of(at * size, size), size)
            low[REACH + at] = fbuf[:, cols].astype(jnp.bfloat16)

    field_copy(0).wait()
    lower(0)
    field_copy(groups - 1).wait()
    lower(groups - 1)

    pl.semaphore_wait(barrier, pairs + jnp.minimum(slab, 1) + jnp.minimum(slabs - 1 - slab, 1))

    to_left = pltpu.make_async_remote_copy(
        src_ref=low.at[pl.ds(REACH, REACH)], dst_ref=low.at[pl.ds(REACH + count, REACH)],
        send_sem=halo_send.at[0], recv_sem=halo_recv.at[0],
        device_id={"mesh": slab - 1}, device_id_type=MESH)
    to_right = pltpu.make_async_remote_copy(
        src_ref=low.at[pl.ds(count, REACH)], dst_ref=low.at[pl.ds(0, REACH)],
        send_sem=halo_send.at[1], recv_sem=halo_recv.at[1],
        device_id={"mesh": slab + 1}, device_id_type=MESH)

    @pl.when(has_left)
    def _():
        to_left.start()

    @pl.when(has_right)
    def _():
        to_right.start()

    @pl.when(jnp.logical_not(has_left))
    def _():
        low[pl.ds(0, REACH)] = jnp.zeros((REACH, rows, size), jnp.bfloat16)

    @pl.when(jnp.logical_not(has_right))
    def _():
        low[pl.ds(REACH + count, REACH)] = jnp.zeros((REACH, rows, size), jnp.bfloat16)

    field_copy(1).wait()
    lower(1)
    weight_copy(1).wait()
    coef_copy.wait()

    def stencil(g, k):
        tall = []
        for b in range(group):
            at = g * group + b
            wide = []
            for c in range(taps):
                keep = jnp.full((rows, size), couplings[c, at].astype(jnp.float32)).astype(jnp.bfloat16)
                wide.append(low[at + c] * keep)
            tall.append(jnp.concatenate(wide, axis=1))
        stacked = jnp.concatenate(tall, axis=0)
        return jnp.dot(stacked, weights[k].reshape(taps * size, size), preferred_element_type=jnp.float32)

    def piece(slot, g):
        return gathered.at[slot, pl.ds(g * group, group)]

    def send(slot, g, target, sem):
        return pltpu.make_async_remote_copy(
            src_ref=piece(slot, g), dst_ref=piece(slot, g), send_sem=sem, recv_sem=recv.at[slot, g],
            device_id={"mode": target}, device_id_type=MESH)

    def turn(t):
        return lax.rem(t + 1, groups)

    @pl.loop(0, groups)
    def _(t):
        g = turn(t)

        @pl.when(t + 2 <= groups - 2)
        def _():
            field_copy(t + 2).wait()
            lower(t + 2)

        @pl.when(jnp.logical_and(t == groups - 2, has_right))
        def _():
            to_left.wait_recv()

        @pl.when(jnp.logical_and(t == groups - 1, has_left))
        def _():
            to_right.wait_recv()

        sums = stencil(g, 1)
        for b in range(group):
            at = g * group + b
            cols = pl.ds(pl.multiple_of(at * size, size), size)
            scaled = sums[b * rows:(b + 1) * rows] * coef[1:2, cols]
            gathered[me, at] = scaled.astype(jnp.bfloat16)
        for j, peer in enumerate(peers):
            send(me, g, peer, far_send.at[j, g]).start()
        send(me, g, sibling, near_send.at[g]).start()

    part, _, links = chaos_values.shape
    total_rows = modes * rows
    per_row = links * part // total_rows
    column_of = lax.broadcasted_iota(jnp.int32, (1, total_rows), 1) // part
    for n in range(links):
        hits[n:n + 1, :] = (column_of == chaos_index[1, n]).astype(jnp.float32)
    lane_of = lax.broadcasted_iota(jnp.int32, (part, total_rows), 1)
    step_of = lax.broadcasted_iota(jnp.int32, (part, total_rows), 0)
    repeat = (lax.rem(lane_of, part) == step_of).astype(jnp.float32).astype(jnp.bfloat16)
    row_of = lax.broadcasted_iota(jnp.int32, (rows, links), 0)
    owner_of = lax.broadcasted_iota(jnp.int32, (rows, links), 1) // per_row
    owned = owner_of == row_of // part + me * (rows // part)
    built = jnp.zeros((rows, total_rows), jnp.float32)
    for i in range(part):
        spread_out = lax.dot_general(
            chaos_values[i], repeat, (((0,), (0,)), ((), ())), preferred_element_type=jnp.float32)
        placed = (spread_out * hits[0:links, :]).astype(jnp.bfloat16)
        mine = jnp.logical_and(owned, lax.rem(row_of, part) == i).astype(jnp.float32).astype(jnp.bfloat16)
        built = built + jnp.dot(mine, placed, preferred_element_type=jnp.float32)
    matrix[...] = built.astype(jnp.bfloat16)

    weight_copy(0).wait()

    @pl.loop(0, groups)
    def _(t):
        g = turn(t)
        right_copy(g).wait()
        sums = stencil(g, 0)
        for b in range(group):
            at = g * group + b
            cols = pl.ds(pl.multiple_of(at * size, size), size)
            rbuf[:, cols] = rbuf[:, cols] - sums[b * rows:(b + 1) * rows] * coef[0:1, cols]

    def mix(g):
        send(sibling, g, sibling, near_send.at[g]).wait_recv()
        for j, peer in enumerate(peers):
            other = peer + 1 - 2 * lax.rem(peer, 2)
            send(other, g, sibling, forward_send.at[j, g]).wait_recv()
        for b in range(group):
            at = g * group + b
            cols = pl.ds(pl.multiple_of(at * size, size), size)
            mixed = jnp.dot(
                matrix[...], gathered[:, at].reshape(modes * rows, size), preferred_element_type=jnp.float32)
            rbuf[:, cols] = rbuf[:, cols] - mixed

    def forward(g):
        for j, peer in enumerate(peers):
            send(peer, g, peer, far_send.at[j, g]).wait_recv()
            send(peer, g, sibling, forward_send.at[j, g]).start()

    forward(turn(0))

    @pl.loop(1, groups)
    def _(t):
        forward(turn(t))
        mix(turn(t - 1))

    mix(turn(groups - 1))

    @pl.loop(0, groups)
    def _(g):
        send(me, g, sibling, near_send.at[g]).wait_send()
        for j, peer in enumerate(peers):
            send(me, g, peer, far_send.at[j, g]).wait_send()
            send(peer, g, sibling, forward_send.at[j, g]).wait_send()

    @pl.when(has_left)
    def _():
        to_left.wait_send()

    @pl.when(has_right)
    def _():
        to_right.wait_send()


def packed_kernel(
    modes, slabs, group, packed,
    field, right, coefficient, blocks, couplings, chaos_values, chaos_index,
    fbuf, rbuf,
    low, weights, coef, gathered, outgoing, arrived, matrix, hits, picks,
    field_sem, right_sem, weight_sem, coef_sem,
    halo_send, halo_recv, near_send, near_recv, far_send, far_recv, forward_send, forward_recv,
):
    rows, width = field.shape
    size = blocks.shape[-1]
    count = width // size
    groups = count // group
    span = group * size
    taps = 2 * REACH + 1
    pairs = modes // 2
    me = lax.axis_index("mode")
    slab = lax.axis_index("mesh")
    sibling = me + 1 - 2 * lax.rem(me, 2)
    peer = lax.rem(me + 2, modes)
    peers = [peer]
    core = lax.rem(me, 2)
    here = me // 2
    there = peer // 2
    share = group // 2
    has_left = slab > 0
    has_right = slab < slabs - 1

    def columns(g):
        return pl.ds(pl.multiple_of(g * span, span), span)

    def field_copy(g):
        return pltpu.make_async_copy(field.at[:, columns(g)], fbuf.at[:, columns(g)], field_sem.at[g])

    def right_copy(g):
        return pltpu.make_async_copy(right.at[:, columns(g)], rbuf.at[:, columns(g)], right_sem.at[g])

    def weight_copy(k):
        return pltpu.make_async_copy(blocks.at[k], weights.at[k], weight_sem.at[k])

    field_copy(0).start()
    field_copy(groups - 1).start()
    weight_copy(1).start()
    coef_copy = pltpu.make_async_copy(coefficient, coef, coef_sem)
    coef_copy.start()

    @pl.loop(1, groups - 1)
    def _(g):
        field_copy(g).start()

    weight_copy(0).start()

    @pl.loop(0, groups)
    def _(g):
        right_copy(g).start()

    barrier = pltpu.get_barrier_semaphore()
    for other in [sibling] + peers:
        pl.semaphore_signal(barrier, inc=1, device_id={"mode": other}, device_id_type=MESH)

    @pl.when(has_left)
    def _():
        pl.semaphore_signal(barrier, inc=1, device_id={"mesh": slab - 1}, device_id_type=MESH)

    @pl.when(has_right)
    def _():
        pl.semaphore_signal(barrier, inc=1, device_id={"mesh": slab + 1}, device_id_type=MESH)

    def lower(g):
        for b in range(group):
            at = g * group + b
            cols = pl.ds(pl.multiple_of(at * size, size), size)
            low[REACH + at] = fbuf[:, cols].astype(jnp.bfloat16)

    part, _, links = chaos_values.shape
    total_rows = modes * rows
    per_row = links * part // total_rows
    column_of = lax.broadcasted_iota(jnp.int32, (1, total_rows), 1) // part
    for n in range(links):
        hits[n:n + 1, :] = (column_of == chaos_index[1, n]).astype(jnp.float32)
    both = 2 * rows
    tall = packed * part
    lanes = lax.broadcasted_iota(jnp.int32, (1, total_rows), 1)
    pair_of_entry = lax.broadcasted_iota(jnp.int32, (links, total_rows), 0) // per_row * part // both
    earlier = jnp.logical_and(
        lax.broadcasted_iota(jnp.int32, (total_rows, total_rows), 0) // part
        < lax.broadcasted_iota(jnp.int32, (total_rows, total_rows), 1) // part,
        jnp.logical_and(
            lax.broadcasted_iota(jnp.int32, (total_rows, total_rows), 0) // both
            == lax.broadcasted_iota(jnp.int32, (total_rows, total_rows), 1) // both,
            lax.rem(lax.broadcasted_iota(jnp.int32, (total_rows, total_rows), 0), part) == 0))
    earlier = earlier.astype(jnp.float32).astype(jnp.bfloat16)

    def picked(source, target):
        wanted = jnp.max(jnp.where(pair_of_entry == target, hits[0:links, :], 0.0), axis=0, keepdims=True)
        wanted = jnp.where(lanes // both == source, wanted, 0.0)
        before = jnp.dot(
            jnp.broadcast_to(wanted, (8, total_rows)).astype(jnp.bfloat16), earlier,
            preferred_element_type=jnp.float32)[0:1]
        place = before * part + lax.rem(lanes, part).astype(jnp.float32)
        row = lax.broadcasted_iota(jnp.int32, (tall, total_rows), 0).astype(jnp.float32)
        return jnp.where(jnp.logical_and(row == place, wanted > 0.0), 1.0, 0.0).astype(jnp.bfloat16)

    picks[...] = picked(here, there)

    field_copy(0).wait()
    lower(0)
    field_copy(groups - 1).wait()
    lower(groups - 1)

    pl.semaphore_wait(barrier, pairs + jnp.minimum(slab, 1) + jnp.minimum(slabs - 1 - slab, 1))

    to_left = pltpu.make_async_remote_copy(
        src_ref=low.at[pl.ds(REACH, REACH)], dst_ref=low.at[pl.ds(REACH + count, REACH)],
        send_sem=halo_send.at[0], recv_sem=halo_recv.at[0],
        device_id={"mesh": slab - 1}, device_id_type=MESH)
    to_right = pltpu.make_async_remote_copy(
        src_ref=low.at[pl.ds(count, REACH)], dst_ref=low.at[pl.ds(0, REACH)],
        send_sem=halo_send.at[1], recv_sem=halo_recv.at[1],
        device_id={"mesh": slab + 1}, device_id_type=MESH)

    @pl.when(has_left)
    def _():
        to_left.start()

    @pl.when(has_right)
    def _():
        to_right.start()

    @pl.when(jnp.logical_not(has_left))
    def _():
        low[pl.ds(0, REACH)] = jnp.zeros((REACH, rows, size), jnp.bfloat16)

    @pl.when(jnp.logical_not(has_right))
    def _():
        low[pl.ds(REACH + count, REACH)] = jnp.zeros((REACH, rows, size), jnp.bfloat16)

    field_copy(1).wait()
    lower(1)
    weight_copy(1).wait()
    coef_copy.wait()

    def stencil(g, k):
        tall = []
        for b in range(group):
            at = g * group + b
            wide = []
            for c in range(taps):
                keep = jnp.full((rows, size), couplings[c, at].astype(jnp.float32)).astype(jnp.bfloat16)
                wide.append(low[at + c] * keep)
            tall.append(jnp.concatenate(wide, axis=1))
        stacked = jnp.concatenate(tall, axis=0)
        return jnp.dot(stacked, weights[k].reshape(taps * size, size), preferred_element_type=jnp.float32)

    def near(g):
        held = gathered.at[core, pl.ds(g * group, group)]
        return pltpu.make_async_remote_copy(
            src_ref=held, dst_ref=held, send_sem=near_send.at[g], recv_sem=near_recv.at[g],
            device_id={"mode": sibling}, device_id_type=MESH)

    def far(g):
        return pltpu.make_async_remote_copy(
            src_ref=outgoing.at[pl.ds(g * share, share)],
            dst_ref=arrived.at[pl.ds(g * group + core * share, share)],
            send_sem=far_send.at[g], recv_sem=far_recv.at[g],
            device_id={"mode": peer}, device_id_type=MESH)

    def relay(g):
        held = arrived.at[pl.ds(g * group + core * share, share)]
        return pltpu.make_async_remote_copy(
            src_ref=held, dst_ref=held, send_sem=forward_send.at[g], recv_sem=forward_recv.at[g],
            device_id={"mode": sibling}, device_id_type=MESH)

    def pack(g):
        near(g).wait_recv()
        chosen = picks[:, pl.ds(pl.multiple_of(here * both, both), both)]
        for b in range(share):
            at = g * group + core * share + b
            outgoing[g * share + b] = jnp.dot(
                chosen, gathered[:, at].reshape(both, size),
                preferred_element_type=jnp.float32).astype(jnp.bfloat16)
        far(g).start()

    def turn(t):
        return lax.rem(t + 1, groups)

    @pl.loop(0, groups)
    def _(t):
        g = turn(t)

        @pl.when(t + 2 <= groups - 2)
        def _():
            field_copy(t + 2).wait()
            lower(t + 2)

        @pl.when(jnp.logical_and(t == groups - 2, has_right))
        def _():
            to_left.wait_recv()

        @pl.when(jnp.logical_and(t == groups - 1, has_left))
        def _():
            to_right.wait_recv()

        sums = stencil(g, 1)
        for b in range(group):
            at = g * group + b
            cols = pl.ds(pl.multiple_of(at * size, size), size)
            scaled = sums[b * rows:(b + 1) * rows] * coef[1:2, cols]
            gathered[core, at] = scaled.astype(jnp.bfloat16)
        near(g).start()

        @pl.when(t > 0)
        def _():
            pack(turn(t - 1))

    pack(turn(groups - 1))

    lane_of = lax.broadcasted_iota(jnp.int32, (part, total_rows), 1)
    step_of = lax.broadcasted_iota(jnp.int32, (part, total_rows), 0)
    repeat = (lax.rem(lane_of, part) == step_of).astype(jnp.float32).astype(jnp.bfloat16)
    row_of = lax.broadcasted_iota(jnp.int32, (rows, links), 0)
    owner_of = lax.broadcasted_iota(jnp.int32, (rows, links), 1) // per_row
    owned = owner_of == row_of // part + me * (rows // part)
    built = jnp.zeros((rows, total_rows), jnp.float32)
    for i in range(part):
        spread_out = lax.dot_general(
            chaos_values[i], repeat, (((0,), (0,)), ((), ())), preferred_element_type=jnp.float32)
        placed = (spread_out * hits[0:links, :]).astype(jnp.bfloat16)
        mine = jnp.logical_and(owned, lax.rem(row_of, part) == i).astype(jnp.float32).astype(jnp.bfloat16)
        built = built + jnp.dot(mine, placed, preferred_element_type=jnp.float32)
    built = built.astype(jnp.bfloat16)
    matrix[:, both:both + tall] = lax.dot_general(
        built, picked(there, here), (((1,), (1,)), ((), ())),
        preferred_element_type=jnp.float32).astype(jnp.bfloat16)
    hits[0:rows, :] = built.astype(jnp.float32)
    matrix[:, 0:both] = hits[0:rows, pl.ds(pl.multiple_of(here * both, both), both)].astype(jnp.bfloat16)

    weight_copy(0).wait()

    @pl.loop(0, groups)
    def _(t):
        g = turn(t)
        right_copy(g).wait()
        sums = stencil(g, 0)
        for b in range(group):
            at = g * group + b
            cols = pl.ds(pl.multiple_of(at * size, size), size)
            rbuf[:, cols] = rbuf[:, cols] - sums[b * rows:(b + 1) * rows] * coef[0:1, cols]

    def mix(g):
        relay(g).wait_recv()
        for b in range(group):
            at = g * group + b
            cols = pl.ds(pl.multiple_of(at * size, size), size)
            stacked = jnp.concatenate([gathered[:, at].reshape(both, size), arrived[at]], axis=0)
            mixed = jnp.dot(matrix[...], stacked, preferred_element_type=jnp.float32)
            rbuf[:, cols] = rbuf[:, cols] - mixed

    def forward(g):
        far(g).wait_recv()
        relay(g).start()

    forward(turn(0))

    @pl.loop(1, groups)
    def _(t):
        forward(turn(t))
        mix(turn(t - 1))

    mix(turn(groups - 1))

    @pl.loop(0, groups)
    def _(g):
        near(g).wait_send()
        far(g).wait_send()
        relay(g).wait_send()

    @pl.when(has_left)
    def _():
        to_left.wait_send()

    @pl.when(has_right)
    def _():
        to_right.wait_send()


def finish_kernel(pieces, field, found, precond, updated, residual, stage, sems):
    rows, width = field.shape
    span = width // pieces

    def columns(i):
        return pl.ds(pl.multiple_of(i * span, span), span)

    def found_copy(i):
        return pltpu.make_async_copy(found.at[:, columns(i)], residual.at[:, columns(i)], sems.at[0, i])

    def stage_copy(i):
        return pltpu.make_async_copy(stage.at[:, columns(i)], updated.at[:, columns(i)], sems.at[1, i])

    @pl.loop(0, pieces)
    def _(i):
        found_copy(i).start()
        cols = columns(i)
        stage[:, cols] = field[:, cols] + precond[:, cols] * found[:, cols]
        stage_copy(i).start()

    @pl.loop(0, pieces)
    def _(i):
        found_copy(i).wait()
        stage_copy(i).wait()


def choose_kernel(held, fewest, chaos_index, choice):
    entries = chaos_index.shape[1]
    seen = jnp.int32(0)
    for n in range(entries):
        column = chaos_index[1, n]
        crosses = column // held != n * 2 * held // entries // held
        seen = seen | jnp.where(crosses, jnp.int32(1) << column, 0)
    counts = [sum((seen >> (side * held + i)) & 1 for i in range(held)) for side in range(2)]
    choice[0, 0] = jnp.maximum(jnp.maximum(counts[0], counts[1]) - fewest, 0)


def shards(modes, slabs, field, right_side, coefficient, precond, blocks, couplings, chaos_values, chaos_index):
    rows, width = field.shape
    size = blocks.shape[-1]
    taps = blocks.shape[1]
    count = width // size
    group = 4
    groups = count // group
    others = max(modes // 2 - 1, 1)
    inside = pl.BlockSpec(memory_space=pltpu.VMEM)
    anywhere = pl.BlockSpec(memory_space=pl.ANY)
    spare = 67043328 - 2 * rows * width * 4 - 96 * 1024
    scalars = pl.BlockSpec(memory_space=pltpu.SMEM)
    dma = pltpu.SemaphoreType.DMA
    part = chaos_values.shape[1]
    both = 2 * rows
    entries = chaos_values.shape[0]
    common = [
        pltpu.VMEM((count + 2 * REACH, rows, size), jnp.bfloat16),
        pltpu.VMEM(blocks.shape, jnp.bfloat16),
        pltpu.VMEM(coefficient.shape, jnp.float32),
    ]
    waits = [dma((groups,)), dma((groups,)), dma((2,)), dma, dma((2,)), dma((2,))]
    hits = pltpu.VMEM((max(entries, rows), modes * rows), jnp.float32)

    def whole(*operands):
        return run(
            functools.partial(kernel, modes, slabs, group), 0,
            common + [
                pltpu.VMEM((modes, count, rows, size), jnp.bfloat16),
                pltpu.VMEM((rows, modes * rows), jnp.bfloat16),
                hits,
            ] + waits + [dma((groups,)), dma((others, groups)), dma((others, groups)), dma((modes, groups))],
            operands)

    def reduced(packed, *operands):
        tall = packed * part
        return run(
            functools.partial(packed_kernel, modes, slabs, group, packed), packed,
            common + [
                pltpu.VMEM((2, count, rows, size), jnp.bfloat16),
                pltpu.VMEM((count // 2, tall, size), jnp.bfloat16),
                pltpu.VMEM((count, tall, size), jnp.bfloat16),
                pltpu.VMEM((rows, both + tall), jnp.bfloat16),
                hits,
                pltpu.VMEM((tall, modes * rows), jnp.bfloat16),
            ] + waits + [dma((groups,))] * 6,
            operands)

    def run(body, ident, scratch, operands):
        kept, found = pl.pallas_call(
            body,
            out_shape=[pltpu.VMEM((rows, width), jnp.float32)] * 2,
            in_specs=[anywhere, anywhere, anywhere, anywhere, scalars, inside, scalars],
            out_specs=[inside] * 2,
            scratch_shapes=scratch,
            compiler_params=pltpu.CompilerParams(
                collective_id=ident, has_side_effects=True, vmem_limit_bytes=spare),
            name="gather_mix",
        )(*operands[1:])
        pieces = 16
        return tuple(pl.pallas_call(
            functools.partial(finish_kernel, pieces),
            out_shape=[jax.ShapeDtypeStruct((rows, width), jnp.float32)] * 2,
            in_specs=[inside] * 3,
            out_specs=[anywhere] * 2,
            scratch_shapes=[pltpu.VMEM((rows, width), jnp.float32), dma((2, pieces))],
            compiler_params=pltpu.CompilerParams(vmem_limit_bytes=8 * 1024 * 1024),
            name="finish",
        )(kept, found, operands[0]))

    operands = (
        precond[None, :], field, right_side, coefficient, blocks, couplings.T,
        chaos_values.transpose(1, 2, 0), chaos_index.T)
    if modes != 4 or both % part:
        return whole(*operands)
    held = both // part
    fewest = held // 2 + 1
    choice = pl.pallas_call(
        functools.partial(choose_kernel, held, fewest),
        out_shape=jax.ShapeDtypeStruct((1, 1), jnp.int32),
        in_specs=[scalars],
        out_specs=scalars,
        name="choose",
    )(operands[-1])
    return lax.switch(
        choice[0, 0],
        [functools.partial(reduced, packed) for packed in range(fewest, held + 1)],
        *operands)


def solution(mesh):
    placed = (
        P("mode", "mesh"),
        P("mode", "mesh"),
        P(None, "mesh"),
        P("mesh"),
        P(),
        P("mesh", None),
        P(),
        P(),
    )
    return jax.shard_map(
        functools.partial(shards, mesh.shape["mode"], mesh.shape["mesh"]),
        mesh=mesh,
        in_specs=placed,
        out_specs=(P("mode", "mesh"), P("mode", "mesh")),
        check_vma=False,
    )
```

profile of v0, /device:TPU:0, one launch (start us, length us, event | category | flops | bytes accessed | tf_op | source)
XLA Modules:
  0.0 56.2 jit_solution(8707345591128987351)
XLA Ops:
  0.6 1.5 %choose.1 = s32[1,1]{1,0:T(1,128)} custom-call(s32[2,48]{1,0:T(2,128)} %bitcast.20), custom_call_target="tpu_custom_call" | custom-call | tf_op jit(solution)/shard_map/choose/pallas_call | solution.py:643
  2.8 53.5 %conditional.1 = ((f32[64,16384]{1,0:T(8,128)}, f32[64,16384]{1,0:T(8,128)})) conditional(s32[]{:T(128)} %bitcast.5, (f32[64,16384]{1,0:T(8,128)}, f32[64,16384]{1,0:T(8,128)}, f32[2,16384]{1,0:T(2,128)}, bf16[2,7,256,256]{3,2,1,0:T(8,128)(2,1)}, s32[7,64]{1,0:T(8,128)}, /*index=5*/bf16[16,16,48]{2,1,0:T(8,128)(2,1)}, ...), branch_computations={%region_0.0_spmd, %region_1.0_spmd, %region_2.0_spmd, %region_3.0_... | conditional | bytes 262180 | solution.py:650
  2.8 0.0 copy-start.2
  2.8 49.9 %gather_mix.6 = (f32[64,16384]{1,0:T(8,128)S(1)}, f32[64,16384]{1,0:T(8,128)S(1)}) custom-call(f32[64,16384]{1,0:T(8,128)} %get-tuple-element.138.field, f32[64,16384]{1,0:T(8,128)} %get-tuple-element.142.right, f32[2,16384]{1,0:T(2,128)} %get-tuple-element.146.coefficient, bf16[2,7,256,256]{3,2,1,0:T(8,128)(2,1)} %get-tuple-element.150.blocks, ...), custom_call_target="tpu_custom_call" | custom-call | tf_op jit(solution)/shard_map/cond/branch_2_fun/gather_mix/pallas_call | solution.py:615
  52.7 0.0 copy-done.2
  52.7 3.5 %finish.6 = (f32[64,16384]{1,0:T(8,128)}, f32[64,16384]{1,0:T(8,128)}) custom-call(f32[64,16384]{1,0:T(8,128)S(1)} %get-tuple-element.91.field, f32[64,16384]{1,0:T(8,128)S(1)} %get-tuple-element.92.found, f32[1,16384]{1,0:T(1,128)S(1)} %bitcast.14), custom_call_target="tpu_custom_call" | custom-call | tf_op jit(solution)/shard_map/cond/branch_2_fun/finish/pallas_call | solution.py:626
Async XLA Ops:
  2.8 49.9 %copy-start.2 = (f32[16384]{0:T(1024)S(1)}, f32[16384]{0:T(1024)}, u32[]{:S(2)}) copy-start(f32[16384]{0:T(1024)} %get-tuple-element.158) | copy-start | bytes 196612 | tf_op jit(solution)/shard_map/cond
where the time goes:
time: 56.4 us; the launch traced here: 56.2 us
  Pallas kernels  54.9 us (97%)
  between operations  1.29 us (2%)
    pallas_call x1, Pallas kernels, run(): pl.pallas_call(body, out_shape=[pltpu.VMEM((rows, width), jnp.float32)] *...  49.9 us
    pallas_call x1, Pallas kernels, run(): pl.pallas_call(functools.partial(finish_kernel, pieces), out_shape=[jax.S...  3.54 us
    pallas_call x1, Pallas kernels, shards(): pl.pallas_call(functools.partial(choose_kernel, held, fewest), out_shape=...  1.49 us

commit v1 on v0

--- a/solution.py
+++ b/solution.py
@@ -241,13 +241,122 @@
         to_right.wait_send()
 
 
+def masked_stencil(low, base, couplings, at, group, weights, taps, size):
+    rows = low.shape[1]
+    tall = []
+    for b in range(group):
+        wide = []
+        for c in range(taps):
+            keep = jnp.full((rows, size), couplings[c, at + b].astype(jnp.float32)).astype(jnp.bfloat16)
+            wide.append(low[base + b + c] * keep)
+        tall.append(jnp.concatenate(wide, axis=1))
+    stacked = jnp.concatenate(tall, axis=0)
+    return jnp.dot(stacked, weights.reshape(taps * size, size), preferred_element_type=jnp.float32)
+
+
+def cheapest_cover(held, adjacent):
+    chosen = lax.broadcasted_iota(jnp.int32, (8, 128), 0) * 128 + lax.broadcasted_iota(jnp.int32, (8, 128), 1)
+    rest = chosen ^ (2 ** held - 1)
+    columns = sum((chosen >> i) & 1 for i in range(held))
+    uncovered = sum(jnp.where((rest & links) != 0, 1, 0) for links in adjacent)
+    key = ((columns + uncovered) << (held + 4)) + (uncovered << held) + chosen
+    key = jnp.where(chosen < 2 ** held, key.astype(jnp.float32), float(2 ** 23))
+    return jnp.min(key).astype(jnp.int32)
+
+
+def slots_of(held, chosen, adjacent):
+    used = jnp.int32(0)
+    columns = []
+    for c in range(held):
+        taken = (chosen >> c) & 1
+        columns.append(jnp.where(taken == 1, used, -1))
+        used = used + taken
+    rows = []
+    for links in adjacent:
+        taken = jnp.where((links & ~chosen) != 0, 1, 0)
+        rows.append(jnp.where(taken == 1, used, -1))
+        used = used + taken
+    return columns, rows
+
+
+def along(shape, axis, shift, values):
+    block = lax.broadcasted_iota(jnp.int32, shape, axis) >> shift
+    found = jnp.full(shape, -1, jnp.int32)
+    for i, value in enumerate(values):
+        found = jnp.where(block == i, value, found)
+    return found
+
+
+def choose_kernel(
+    group, fewest,
+    field, coefficient, precond, blocks, chaos_values, chaos_index, index_row,
+    choice, slots, weights, first, coef, scale, placed,
+    values, wide_index, links_smem, sems,
+):
+    size = blocks.shape[-1]
+    part, _, entries = chaos_values.shape
+    total = placed.shape[1]
+    held = total // part // 2
+    shift = held.bit_length() - 1
+    per_row = entries // (2 * held)
+    near_span = pl.ds((group - REACH) * size, (group + 2 * REACH) * size)
+    copies = [
+        pltpu.make_async_copy(chaos_index, links_smem, sems.at[0]),
+        pltpu.make_async_copy(index_row, wide_index, sems.at[1]),
+        pltpu.make_async_copy(chaos_values, values, sems.at[2]),
+        pltpu.make_async_copy(blocks.at[1], weights, sems.at[3]),
+        pltpu.make_async_copy(field.at[:, near_span], first, sems.at[4]),
+        pltpu.make_async_copy(coefficient, coef, sems.at[5]),
+        pltpu.make_async_copy(precond, scale, sems.at[6]),
+    ]
+    for copy in copies:
+        copy.start()
+
+    copies[0].wait()
+    adjacent = [[], []]
+    for row in range(2 * held):
+        side = row // held
+        links = jnp.int32(0)
+        for n in range(row * per_row, row * per_row + per_row):
+            column = links_smem[1, n]
+            links = links | (((column >> shift) ^ side) << (column & (held - 1)))
+        adjacent[side].append(links)
+    best = [cheapest_cover(held, links) for links in adjacent]
+    needed = jnp.maximum(best[0] >> (held + 4), best[1] >> (held + 4))
+    choice[0, 0] = jnp.maximum(needed - fewest, 0)
+    for side in range(2):
+        columns, rows = slots_of(held, best[side] & (2 ** held - 1), adjacent[side])
+        for i, value in enumerate(columns + rows):
+            slots[0, side * 2 * held + i] = value
+
+    copies[1].wait()
+    copies[2].wait()
+    square = (entries, entries)
+    wide_row = jnp.broadcast_to(wide_index[1:2, :], square).astype(jnp.float32)
+    eye = lax.broadcasted_iota(jnp.int32, square, 0) == lax.broadcasted_iota(jnp.int32, square, 1)
+    column_of = jnp.sum(jnp.where(eye, wide_row, 0.0), axis=1, keepdims=True)
+    step = part.bit_length() - 1
+    lane_block = (lax.broadcasted_iota(jnp.int32, (entries, total), 1) >> step).astype(jnp.float32)
+    hits = (lane_block == column_of).astype(jnp.float32)
+    lane_of = lax.broadcasted_iota(jnp.int32, (part, total), 1)
+    step_of = lax.broadcasted_iota(jnp.int32, (part, total), 0)
+    repeat = ((lane_of & (part - 1)) == step_of).astype(jnp.float32).astype(jnp.bfloat16)
+    for i in range(part):
+        spread_out = lax.dot_general(
+            values[i], repeat, (((0,), (0,)), ((), ())), preferred_element_type=jnp.float32)
+        placed[i * entries:(i + 1) * entries] = (spread_out * hits).astype(jnp.bfloat16)
+
+    for copy in copies[3:]:
+        copy.wait()
+
+
 def packed_kernel(
-    modes, slabs, group, packed,
-    field, right, coefficient, blocks, couplings, chaos_values, chaos_index,
+    modes, slabs, group, entries, packed,
+    field, right, blocks, couplings, slots, early, first, coef, scale, placed,
     fbuf, rbuf,
-    low, weights, coef, gathered, outgoing, arrived, matrix, hits, picks,
-    field_sem, right_sem, weight_sem, coef_sem,
-    halo_send, halo_recv, near_send, near_recv, far_send, far_recv, forward_send, forward_recv,
+    low, later, gathered, outgoing, arrived, picks, matrix, links, slot_of,
+    load_sem, field_sem, halo_send, halo_recv,
+    near_send, near_recv, far_send, far_recv, forward_send, forward_recv,
 ):
     rows, width = field.shape
     size = blocks.shape[-1]
@@ -256,48 +365,26 @@
     span = group * size
     taps = 2 * REACH + 1
     pairs = modes // 2
+    both = 2 * rows
+    total = 2 * both
+    part = picks.shape[0] // packed
+    held = both // part
+    shift = part.bit_length() - 1
+    per_row = entries // (2 * held)
+    tall = packed * part
     me = lax.axis_index("mode")
     slab = lax.axis_index("mesh")
     sibling = me + 1 - 2 * lax.rem(me, 2)
     peer = lax.rem(me + 2, modes)
-    peers = [peer]
     core = lax.rem(me, 2)
     here = me // 2
-    there = peer // 2
     share = group // 2
+    batch = groups // 4
     has_left = slab > 0
     has_right = slab < slabs - 1
 
-    def columns(g):
-        return pl.ds(pl.multiple_of(g * span, span), span)
-
-    def field_copy(g):
-        return pltpu.make_async_copy(field.at[:, columns(g)], fbuf.at[:, columns(g)], field_sem.at[g])
-
-    def right_copy(g):
-        return pltpu.make_async_copy(right.at[:, columns(g)], rbuf.at[:, columns(g)], right_sem.at[g])
-
-    def weight_copy(k):
-        return pltpu.make_async_copy(blocks.at[k], weights.at[k], weight_sem.at[k])
-
-    field_copy(0).start()
-    field_copy(groups - 1).start()
-    weight_copy(1).start()
-    coef_copy = pltpu.make_async_copy(coefficient, coef, coef_sem)
-    coef_copy.start()
-
-    @pl.loop(1, groups - 1)
-    def _(g):
-        field_copy(g).start()
-
-    weight_copy(0).start()
-
-    @pl.loop(0, groups)
-    def _(g):
-        right_copy(g).start()
-
     barrier = pltpu.get_barrier_semaphore()
-    for other in [sibling] + peers:
+    for other in [sibling, peer]:
         pl.semaphore_signal(barrier, inc=1, device_id={"mode": other}, device_id_type=MESH)
 
     @pl.when(has_left)
@@ -308,49 +395,120 @@
     def _():
         pl.semaphore_signal(barrier, inc=1, device_id={"mesh": slab + 1}, device_id_type=MESH)
 
+    def field_copy(q):
+        cols = pl.ds(pl.multiple_of(q * batch * span, span), batch * span)
+        return pltpu.make_async_copy(field.at[:, cols], fbuf.at[:, cols], field_sem.at[q])
+
+    links_copy = pltpu.make_async_copy(couplings, links, load_sem.at[0])
+    slots_copy = pltpu.make_async_copy(slots, slot_of, load_sem.at[1])
+    later_copy = pltpu.make_async_copy(blocks.at[0], later, load_sem.at[2])
+    right_copy = pltpu.make_async_copy(right, rbuf, load_sem.at[3])
+    links_copy.start()
+    slots_copy.start()
+    for q in (0, 3, 1, 2):
+        field_copy(q).start()
+    later_copy.start()
+    right_copy.start()
+
+    def lower_block(at):
+        cols = pl.ds(pl.multiple_of(at * size, size), size)
+        low[REACH + at] = fbuf[:, cols].astype(jnp.bfloat16)
+
     def lower(g):
+        for b in range(group):
+            lower_block(g * group + b)
+
+    def near(g):
+        ours = gathered.at[core, pl.ds(g * group, group)]
+        return pltpu.make_async_remote_copy(
+            src_ref=ours, dst_ref=ours, send_sem=near_send, recv_sem=near_recv.at[g],
+            device_id={"mode": sibling}, device_id_type=MESH)
+
+    def far(g):
+        return pltpu.make_async_remote_copy(
+            src_ref=outgoing.at[pl.ds(g * share, share)],
+            dst_ref=arrived.at[pl.ds(g * group + core * share, share)],
+            send_sem=far_send, recv_sem=far_recv.at[g],
+            device_id={"mode": peer}, device_id_type=MESH)
+
+    def relay(g):
+        ours = arrived.at[pl.ds(g * group + core * share, share)]
+        return pltpu.make_async_remote_copy(
+            src_ref=ours, dst_ref=ours, send_sem=forward_send, recv_sem=forward_recv.at[g],
+            device_id={"mode": sibling}, device_id_type=MESH)
+
+    def pack(g):
+        near(g).wait_recv()
+        for b in range(share):
+            at = g * group + core * share + b
+            outgoing[g * share + b] = jnp.dot(
+                picks[...], gathered[:, at].reshape(both, size),
+                preferred_element_type=jnp.float32).astype(jnp.bfloat16)
+        far(g).start()
+
+    def turn(t):
+        return lax.rem(t + 1, groups)
+
+    def stencil(g, weights):
+        return masked_stencil(low, g * group, links, g * group, group, weights[...], taps, size)
+
+    def spread(g):
+        sums = stencil(g, early)
         for b in range(group):
             at = g * group + b
             cols = pl.ds(pl.multiple_of(at * size, size), size)
-            low[REACH + at] = fbuf[:, cols].astype(jnp.bfloat16)
-
-    part, _, links = chaos_values.shape
-    total_rows = modes * rows
-    per_row = links * part // total_rows
-    column_of = lax.broadcasted_iota(jnp.int32, (1, total_rows), 1) // part
-    for n in range(links):
-        hits[n:n + 1, :] = (column_of == chaos_index[1, n]).astype(jnp.float32)
-    both = 2 * rows
-    tall = packed * part
-    lanes = lax.broadcasted_iota(jnp.int32, (1, total_rows), 1)
-    pair_of_entry = lax.broadcasted_iota(jnp.int32, (links, total_rows), 0) // per_row * part // both
-    earlier = jnp.logical_and(
-        lax.broadcasted_iota(jnp.int32, (total_rows, total_rows), 0) // part
-        < lax.broadcasted_iota(jnp.int32, (total_rows, total_rows), 1) // part,
-        jnp.logical_and(
-            lax.broadcasted_iota(jnp.int32, (total_rows, total_rows), 0) // both
-            == lax.broadcasted_iota(jnp.int32, (total_rows, total_rows), 1) // both,
-            lax.rem(lax.broadcasted_iota(jnp.int32, (total_rows, total_rows), 0), part) == 0))
-    earlier = earlier.astype(jnp.float32).astype(jnp.bfloat16)
-
-    def picked(source, target):
-        wanted = jnp.max(jnp.where(pair_of_entry == target, hits[0:links, :], 0.0), axis=0, keepdims=True)
-        wanted = jnp.where(lanes // both == source, wanted, 0.0)
-        before = jnp.dot(
-            jnp.broadcast_to(wanted, (8, total_rows)).astype(jnp.bfloat16), earlier,
-            preferred_element_type=jnp.float32)[0:1]
-        place = before * part + lax.rem(lanes, part).astype(jnp.float32)
-        row = lax.broadcasted_iota(jnp.int32, (tall, total_rows), 0).astype(jnp.float32)
-        return jnp.where(jnp.logical_and(row == place, wanted > 0.0), 1.0, 0.0).astype(jnp.bfloat16)
-
-    picks[...] = picked(here, there)
+            scaled = sums[b * rows:(b + 1) * rows] * coef[1:2, cols]
+            gathered[core, at] = scaled.astype(jnp.bfloat16)
+
+    for b in range(group + 2 * REACH):
+        low[group + b] = first[:, b * size:(b + 1) * size].astype(jnp.bfloat16)
+    links_copy.wait()
+    spread(1)
+    pl.semaphore_wait(barrier, pairs + jnp.minimum(slab, 1) + jnp.minimum(slabs - 1 - slab, 1))
+    near(1).start()
+
+    slots_copy.wait()
+    lane = lax.broadcasted_iota(jnp.int32, (1, part * entries), 1)
+    lane_step = lax.div(lane, entries)
+    lane_key = lane_step * 2 * held + lax.div(lane - lane_step * entries, per_row)
+
+    def matrix_rows(height, start):
+        row = lax.broadcasted_iota(jnp.int32, (height, 1), 0)
+        row_key = (row & (part - 1)) * 2 * held + (row >> shift) + start
+        wanted = (row_key == lane_key).astype(jnp.float32).astype(jnp.bfloat16)
+        return jnp.dot(wanted, placed[...], preferred_element_type=jnp.float32)
+
+    def half(values, side):
+        return jnp.where(side == 0, values[:, 0:both], values[:, both:total])
+
+    def slots_to(side, kind):
+        first_slot = [slot_of[0, kind * held + i] for i in range(held)]
+        other_slot = [slot_of[0, (2 + kind) * held + i] for i in range(held)]
+        return [jnp.where(side == 0, a, b) for a, b in zip(first_slot, other_slot)]
+
+    def chosen_rows(height, values):
+        row = lax.broadcasted_iota(jnp.int32, (height, both), 0)
+        column = lax.broadcasted_iota(jnp.int32, (height, both), 1)
+        same = (row & (part - 1)) == (column & (part - 1))
+        slot = along((1, both), 1, shift, values)
+        return slot, jnp.logical_and((row >> shift) == slot, same).astype(jnp.float32)
+
+    column_slot, taken = chosen_rows(tall, slots_to(1 - here, 0))
+    _, summed = chosen_rows(tall, slots_to(1 - here, 1))
+    outward = half(matrix_rows(both, (1 - here) * held), here)
+    outward = jnp.where(column_slot < 0, outward, 0.0).astype(jnp.bfloat16)
+    picks[...] = (taken + jnp.dot(
+        summed.astype(jnp.bfloat16), outward, preferred_element_type=jnp.float32)).astype(jnp.bfloat16)
+    pack(1)
 
     field_copy(0).wait()
-    lower(0)
-    field_copy(groups - 1).wait()
+    lower_block(0)
+    for at in range(group + 2 * REACH + 1, 4 * group):
+        lower_block(at)
+    spread(2)
+    near(2).start()
+    field_copy(3).wait()
     lower(groups - 1)
-
-    pl.semaphore_wait(barrier, pairs + jnp.minimum(slab, 1) + jnp.minimum(slabs - 1 - slab, 1))
 
     to_left = pltpu.make_async_remote_copy(
         src_ref=low.at[pl.ds(REACH, REACH)], dst_ref=low.at[pl.ds(REACH + count, REACH)],
@@ -378,61 +536,14 @@
         low[pl.ds(REACH + count, REACH)] = jnp.zeros((REACH, rows, size), jnp.bfloat16)
 
     field_copy(1).wait()
-    lower(1)
-    weight_copy(1).wait()
-    coef_copy.wait()
-
-    def stencil(g, k):
-        tall = []
-        for b in range(group):
-            at = g * group + b
-            wide = []
-            for c in range(taps):
-                keep = jnp.full((rows, size), couplings[c, at].astype(jnp.float32)).astype(jnp.bfloat16)
-                wide.append(low[at + c] * keep)
-            tall.append(jnp.concatenate(wide, axis=1))
-        stacked = jnp.concatenate(tall, axis=0)
-        return jnp.dot(stacked, weights[k].reshape(taps * size, size), preferred_element_type=jnp.float32)
-
-    def near(g):
-        held = gathered.at[core, pl.ds(g * group, group)]
-        return pltpu.make_async_remote_copy(
-            src_ref=held, dst_ref=held, send_sem=near_send.at[g], recv_sem=near_recv.at[g],
-            device_id={"mode": sibling}, device_id_type=MESH)
-
-    def far(g):
-        return pltpu.make_async_remote_copy(
-            src_ref=outgoing.at[pl.ds(g * share, share)],
-            dst_ref=arrived.at[pl.ds(g * group + core * share, share)],
-            send_sem=far_send.at[g], recv_sem=far_recv.at[g],
-            device_id={"mode": peer}, device_id_type=MESH)
-
-    def relay(g):
-        held = arrived.at[pl.ds(g * group + core * share, share)]
-        return pltpu.make_async_remote_copy(
-            src_ref=held, dst_ref=held, send_sem=forward_send.at[g], recv_sem=forward_recv.at[g],
-            device_id={"mode": sibling}, device_id_type=MESH)
-
-    def pack(g):
-        near(g).wait_recv()
-        chosen = picks[:, pl.ds(pl.multiple_of(here * both, both), both)]
-        for b in range(share):
-            at = g * group + core * share + b
-            outgoing[g * share + b] = jnp.dot(
-                chosen, gathered[:, at].reshape(both, size),
-                preferred_element_type=jnp.float32).astype(jnp.bfloat16)
-        far(g).start()
-
-    def turn(t):
-        return lax.rem(t + 1, groups)
-
-    @pl.loop(0, groups)
+    field_copy(2).wait()
+
+    @pl.loop(2, groups)
     def _(t):
         g = turn(t)
 
         @pl.when(t + 2 <= groups - 2)
         def _():
-            field_copy(t + 2).wait()
             lower(t + 2)
 
         @pl.when(jnp.logical_and(t == groups - 2, has_right))
@@ -443,79 +554,71 @@
         def _():
             to_right.wait_recv()
 
-        sums = stencil(g, 1)
-        for b in range(group):
-            at = g * group + b
-            cols = pl.ds(pl.multiple_of(at * size, size), size)
-            scaled = sums[b * rows:(b + 1) * rows] * coef[1:2, cols]
-            gathered[core, at] = scaled.astype(jnp.bfloat16)
+        spread(g)
         near(g).start()
-
-        @pl.when(t > 0)
-        def _():
-            pack(turn(t - 1))
+        pack(turn(t - 1))
+
+    mine = matrix_rows(rows, me * (held // 2))
+    _, arriving = chosen_rows(tall, slots_to(here, 0))
+    inward = lax.dot_general(
+        half(mine, 1 - here).astype(jnp.bfloat16), arriving.astype(jnp.bfloat16), (((1,), (1,)), ((), ())),
+        preferred_element_type=jnp.float32)
+    in_rows = slots_to(here, 1)
+    my_slots = [jnp.where(core == 0, in_rows[i], in_rows[i + held // 2]) for i in range(held // 2)]
+    row = lax.broadcasted_iota(jnp.int32, (rows, tall), 0)
+    column = lax.broadcasted_iota(jnp.int32, (rows, tall), 1)
+    own = jnp.logical_and(
+        (column >> shift) == along((rows, 1), 0, shift, my_slots), (row & (part - 1)) == (column & (part - 1)))
+    matrix[:, 0:both] = half(mine, here).astype(jnp.bfloat16)
+    matrix[:, both:both + tall] = (inward + own.astype(jnp.float32)).astype(jnp.bfloat16)
 
     pack(turn(groups - 1))
 
-    lane_of = lax.broadcasted_iota(jnp.int32, (part, total_rows), 1)
-    step_of = lax.broadcasted_iota(jnp.int32, (part, total_rows), 0)
-    repeat = (lax.rem(lane_of, part) == step_of).astype(jnp.float32).astype(jnp.bfloat16)
-    row_of = lax.broadcasted_iota(jnp.int32, (rows, links), 0)
-    owner_of = lax.broadcasted_iota(jnp.int32, (rows, links), 1) // per_row
-    owned = owner_of == row_of // part + me * (rows // part)
-    built = jnp.zeros((rows, total_rows), jnp.float32)
-    for i in range(part):
-        spread_out = lax.dot_general(
-            chaos_values[i], repeat, (((0,), (0,)), ((), ())), preferred_element_type=jnp.float32)
-        placed = (spread_out * hits[0:links, :]).astype(jnp.bfloat16)
-        mine = jnp.logical_and(owned, lax.rem(row_of, part) == i).astype(jnp.float32).astype(jnp.bfloat16)
-        built = built + jnp.dot(mine, placed, preferred_element_type=jnp.float32)
-    built = built.astype(jnp.bfloat16)
-    matrix[:, both:both + tall] = lax.dot_general(
-        built, picked(there, here), (((1,), (1,)), ((), ())),
-        preferred_element_type=jnp.float32).astype(jnp.bfloat16)
-    hits[0:rows, :] = built.astype(jnp.float32)
-    matrix[:, 0:both] = hits[0:rows, pl.ds(pl.multiple_of(here * both, both), both)].astype(jnp.bfloat16)
-
-    weight_copy(0).wait()
+    def forward(g):
+        far(g).wait_recv()
+        relay(g).start()
+
+    later_copy.wait()
+    right_copy.wait()
+    ahead = groups // 2
 
     @pl.loop(0, groups)
     def _(t):
-        g = turn(t)
-        right_copy(g).wait()
-        sums = stencil(g, 0)
+        @pl.when(lax.rem(t, 2) == 0)
+        def _():
+            forward(turn(t // 2))
+
+        sums = stencil(t, later)
         for b in range(group):
-            at = g * group + b
+            at = t * group + b
             cols = pl.ds(pl.multiple_of(at * size, size), size)
             rbuf[:, cols] = rbuf[:, cols] - sums[b * rows:(b + 1) * rows] * coef[0:1, cols]
 
-    def mix(g):
+    @pl.loop(0, groups)
+    def _(t):
+        @pl.when(jnp.logical_and(t + 1 >= ahead, t + 1 < groups))
+        def _():
+            forward(turn(t + 1))
+
+        g = turn(t)
         relay(g).wait_recv()
         for b in range(group):
             at = g * group + b
             cols = pl.ds(pl.multiple_of(at * size, size), size)
             stacked = jnp.concatenate([gathered[:, at].reshape(both, size), arrived[at]], axis=0)
             mixed = jnp.dot(matrix[...], stacked, preferred_element_type=jnp.float32)
-            rbuf[:, cols] = rbuf[:, cols] - mixed
-
-    def forward(g):
-        far(g).wait_recv()
-        relay(g).start()
-
-    forward(turn(0))
-
-    @pl.loop(1, groups)
-    def _(t):
-        forward(turn(t))
-        mix(turn(t - 1))
-
-    mix(turn(groups - 1))
-
-    @pl.loop(0, groups)
-    def _(g):
-        near(g).wait_send()
-        far(g).wait_send()
-        relay(g).wait_send()
+            left = rbuf[:, cols] - mixed
+            rbuf[:, cols] = left
+            fbuf[:, cols] = fbuf[:, cols] + scale[:, cols] * left
+
+    def drain(source, sem, other):
+        pltpu.make_async_remote_copy(
+            src_ref=source, dst_ref=source, send_sem=sem, recv_sem=far_recv.at[0],
+            device_id={"mode": other}, device_id_type=MESH).wait_send()
+
+    drain(gathered.at[core], near_send, sibling)
+    drain(outgoing, far_send, peer)
+    drain(outgoing, forward_send, sibling)
 
     @pl.when(has_left)
     def _():
@@ -524,6 +627,16 @@
     @pl.when(has_right)
     def _():
         to_right.wait_send()
+
+
+def write_kernel(pieces, kept, found, updated, residual, sems):
+    tall = kept.shape[0] // pieces
+    for i in range(pieces):
+        some = pl.ds(i * tall, tall)
+        pltpu.make_async_copy(found.at[some], residual.at[some], sems.at[0]).start()
+        pltpu.make_async_copy(kept.at[some], updated.at[some], sems.at[1]).start()
+    pltpu.make_async_copy(found, residual, sems.at[0]).wait()
+    pltpu.make_async_copy(kept, updated, sems.at[1]).wait()
 
 
 def finish_kernel(pieces, field, found, precond, updated, residual, stage, sems):
@@ -550,17 +663,6 @@
     def _(i):
         found_copy(i).wait()
         stage_copy(i).wait()
-
-
-def choose_kernel(held, fewest, chaos_index, choice):
-    entries = chaos_index.shape[1]
-    seen = jnp.int32(0)
-    for n in range(entries):
-        column = chaos_index[1, n]
-        crosses = column // held != n * 2 * held // entries // held
-        seen = seen | jnp.where(crosses, jnp.int32(1) << column, 0)
-    counts = [sum((seen >> (side * held + i)) & 1 for i in range(held)) for side in range(2)]
-    choice[0, 0] = jnp.maximum(jnp.maximum(counts[0], counts[1]) - fewest, 0)
 
 
 def shards(modes, slabs, field, right_side, coefficient, precond, blocks, couplings, chaos_values, chaos_index):
@@ -585,72 +687,105 @@
         pltpu.VMEM(coefficient.shape, jnp.float32),
     ]
     waits = [dma((groups,)), dma((groups,)), dma((2,)), dma, dma((2,)), dma((2,))]
-    hits = pltpu.VMEM((max(entries, rows), modes * rows), jnp.float32)
-
-    def whole(*operands):
-        return run(
-            functools.partial(kernel, modes, slabs, group), 0,
-            common + [
+    arrays = [pltpu.VMEM((rows, width), jnp.float32)] * 2
+    results = [jax.ShapeDtypeStruct((rows, width), jnp.float32)] * 2
+    weights_row = precond[None, :]
+    links = chaos_index.T
+    values = chaos_values.transpose(1, 2, 0)
+
+    def whole():
+        kept, found = pl.pallas_call(
+            functools.partial(kernel, modes, slabs, group),
+            out_shape=arrays,
+            in_specs=[anywhere, anywhere, anywhere, anywhere, scalars, inside, scalars],
+            out_specs=[inside] * 2,
+            scratch_shapes=common + [
                 pltpu.VMEM((modes, count, rows, size), jnp.bfloat16),
                 pltpu.VMEM((rows, modes * rows), jnp.bfloat16),
-                hits,
+                pltpu.VMEM((max(entries, rows), modes * rows), jnp.float32),
             ] + waits + [dma((groups,)), dma((others, groups)), dma((others, groups)), dma((modes, groups))],
-            operands)
-
-    def reduced(packed, *operands):
-        tall = packed * part
-        return run(
-            functools.partial(packed_kernel, modes, slabs, group, packed), packed,
-            common + [
-                pltpu.VMEM((2, count, rows, size), jnp.bfloat16),
-                pltpu.VMEM((count // 2, tall, size), jnp.bfloat16),
-                pltpu.VMEM((count, tall, size), jnp.bfloat16),
-                pltpu.VMEM((rows, both + tall), jnp.bfloat16),
-                hits,
-                pltpu.VMEM((tall, modes * rows), jnp.bfloat16),
-            ] + waits + [dma((groups,))] * 6,
-            operands)
-
-    def run(body, ident, scratch, operands):
-        kept, found = pl.pallas_call(
-            body,
-            out_shape=[pltpu.VMEM((rows, width), jnp.float32)] * 2,
-            in_specs=[anywhere, anywhere, anywhere, anywhere, scalars, inside, scalars],
-            out_specs=[inside] * 2,
-            scratch_shapes=scratch,
             compiler_params=pltpu.CompilerParams(
-                collective_id=ident, has_side_effects=True, vmem_limit_bytes=spare),
+                collective_id=0, has_side_effects=True, vmem_limit_bytes=spare),
             name="gather_mix",
-        )(*operands[1:])
+        )(field, right_side, coefficient, blocks, couplings.T, values, links)
         pieces = 16
         return tuple(pl.pallas_call(
             functools.partial(finish_kernel, pieces),
-            out_shape=[jax.ShapeDtypeStruct((rows, width), jnp.float32)] * 2,
+            out_shape=results,
             in_specs=[inside] * 3,
             out_specs=[anywhere] * 2,
             scratch_shapes=[pltpu.VMEM((rows, width), jnp.float32), dma((2, pieces))],
             compiler_params=pltpu.CompilerParams(vmem_limit_bytes=8 * 1024 * 1024),
             name="finish",
-        )(kept, found, operands[0]))
-
-    operands = (
-        precond[None, :], field, right_side, coefficient, blocks, couplings.T,
-        chaos_values.transpose(1, 2, 0), chaos_index.T)
-    if modes != 4 or both % part:
-        return whole(*operands)
+        )(kept, found, weights_row))
+
     held = both // part
-    fewest = held // 2 + 1
-    choice = pl.pallas_call(
-        functools.partial(choose_kernel, held, fewest),
-        out_shape=jax.ShapeDtypeStruct((1, 1), jnp.int32),
-        in_specs=[scalars],
-        out_specs=scalars,
+    if modes != 4 or both % part or held != 8 or part & (part - 1) or groups % 4 or groups < 8:
+        return whole()
+    fewest = held // 2
+    near_blocks = group + 2 * REACH
+
+    prepared = pl.pallas_call(
+        functools.partial(choose_kernel, group, fewest),
+        out_shape=[
+            jax.ShapeDtypeStruct((1, 1), jnp.int32),
+            jax.ShapeDtypeStruct((1, 4 * held), jnp.int32),
+            pltpu.VMEM(blocks.shape[1:], jnp.bfloat16),
+            pltpu.VMEM((rows, near_blocks * size), jnp.float32),
+            pltpu.VMEM(coefficient.shape, jnp.float32),
+            pltpu.VMEM((1, width), jnp.float32),
+            pltpu.VMEM((part * entries, 2 * both), jnp.bfloat16),
+        ],
+        in_specs=[anywhere] * 7,
+        out_specs=[scalars, scalars] + [inside] * 5,
+        scratch_shapes=[
+            pltpu.VMEM(values.shape, jnp.bfloat16),
+            pltpu.VMEM(links.shape, jnp.int32),
+            pltpu.SMEM(links.shape, jnp.int32),
+            dma((7,)),
+        ],
+        compiler_params=pltpu.CompilerParams(vmem_limit_bytes=67043328 - 4 * 1024 * 1024),
         name="choose",
-    )(operands[-1])
+    )(field, coefficient, weights_row, blocks, values, links, links)
+
+    def reduced(packed, *operands):
+        tall = packed * part
+        kept, found = pl.pallas_call(
+            functools.partial(packed_kernel, modes, slabs, group, entries, packed),
+            out_shape=arrays,
+            in_specs=[anywhere] * 5 + [inside] * 5,
+            out_specs=[inside] * 2,
+            scratch_shapes=[
+                pltpu.VMEM((count + 2 * REACH, rows, size), jnp.bfloat16),
+                pltpu.VMEM(blocks.shape[1:], jnp.bfloat16),
+                pltpu.VMEM((2, count, rows, size), jnp.bfloat16),
+                pltpu.VMEM((count // 2, tall, size), jnp.bfloat16),
+                pltpu.VMEM((count, tall, size), jnp.bfloat16),
+                pltpu.VMEM((tall, both), jnp.bfloat16),
+                pltpu.VMEM((rows, both + tall), jnp.bfloat16),
+                pltpu.SMEM((taps, count), jnp.int32),
+                pltpu.SMEM((1, 4 * held), jnp.int32),
+                dma((4,)), dma((4,)), dma((2,)), dma((2,)),
+                dma, dma((groups,)), dma, dma((groups,)), dma, dma((groups,)),
+            ],
+            compiler_params=pltpu.CompilerParams(
+                collective_id=packed, has_side_effects=True, vmem_limit_bytes=spare - 4 * 1024 * 1024),
+            name="gather_mix",
+        )(*operands)
+        return tuple(pl.pallas_call(
+            functools.partial(write_kernel, 8),
+            out_shape=results,
+            in_specs=[inside] * 2,
+            out_specs=[anywhere] * 2,
+            scratch_shapes=[dma((2,))],
+            compiler_params=pltpu.CompilerParams(vmem_limit_bytes=8 * 1024 * 1024),
+            name="write",
+        )(kept, found))
+
     return lax.switch(
-        choice[0, 0],
+        prepared[0][0, 0],
         [functools.partial(reduced, packed) for packed in range(fewest, held + 1)],
-        *operands)
+        field, right_side, blocks, couplings.T, *prepared[1:])
 
 
 def solution(mesh):

time: 56.4 us -> 49 us (0.87)
  Pallas kernels: 54.9 us -> 47.4 us
    pallas_call x3, Pallas kernels: 54.9 us -> 47.4 us  [the longest x1 41.8 us: reduced(): pl.pallas_call(functools.partial(packed_kernel, modes, slabs, group, entr...]
where the time goes in v1:
time: 49 us; the launch traced here: 48.7 us
  Pallas kernels  47.4 us (97%)
  between operations  1.32 us (3%)
    pallas_call x1, Pallas kernels, reduced(): pl.pallas_call(functools.partial(packed_kernel, modes, slabs, group, entr...  41.8 us
    pallas_call x1, Pallas kernels, reduced(): pl.pallas_call(functools.partial(write_kernel, 8), out_shape=results, in_...  3.29 us
    pallas_call x1, Pallas kernels, shards(): pl.pallas_call(functools.partial(choose_kernel, group, fewest), out_shape...  2.23 us

profile of v1, /device:TPU:0, one launch (start us, length us, event | category | flops | bytes accessed | tf_op | source)
XLA Modules:
  0.0 48.7 jit_solution(17149323029975818377)
XLA Ops:
  0.6 0.0 copy-start
  0.6 0.0 copy-start.1
  0.7 2.2 %choose.1 = (s32[1,1]{1,0:T(1,128)}, s32[1,32]{1,0:T(1,128)S(1)}, bf16[7,256,256]{2,1,0:T(8,128)(2,1)S(1)}, f32[64,2560]{1,0:T(8,128)S(1)}, f32[2,16384]{1,0:T(2...) custom-call(f32[64,16384]{1,0:T(8,128)} %field.1, f32[2,16384]{1,0:T(2,128)} %coefficient.1, ...), custom_call_target="tpu_custom_call" | custom-call | tf_op jit(solution)/shard_map/choose/pallas_call | solution.py:728
  3.5 0.0 copy-done
  3.5 0.0 copy-done.1
  3.6 45.2 %conditional.1 = ((f32[64,16384]{1,0:T(8,128)}, f32[64,16384]{1,0:T(8,128)})) conditional(s32[]{:T(128)} %bitcast.3, (f32[64,16384]{1,0:T(8,128)}, f32[64,16384]{1,0:T(8,128)}, bf16[2,7,256,256]{3,2,1,0:T(8,128)(2,1)S(1)}, s32[7,64]{1,0:T(8,128)S(1)}, s32[1,32]{1,0:T(1,128)S(1)}, ...), branch_computations={%region_0.0_spmd, %region_1.0_spmd, %region_2.0_spmd, %region_3.0_... | conditional | bytes 8 | solution.py:785
  3.6 41.8 %gather_mix.7 = (f32[64,16384]{1,0:T(8,128)S(1)}, f32[64,16384]{1,0:T(8,128)S(1)}) custom-call(f32[64,16384]{1,0:T(8,128)} %get-tuple-element.124.field, f32[64,16384]{1,0:T(8,128)} %get-tuple-element.195.right, bf16[2,7,256,256]{3,2,1,0:T(8,128)(2,1)S(1)} %get-tuple-element.126.blocks, s32[7,64]{1,0:T(8,128)S(1)} %get-tuple-element.127.couplings, ...), custom_call_target="tpu_custom_call" | custom-call | tf_op jit(solution)/shard_map/cond/branch_2_fun/gather_mix/pallas_call | solution.py:753
  45.4 3.3 %write.7 = (f32[64,16384]{1,0:T(8,128)}, f32[64,16384]{1,0:T(8,128)}) custom-call(f32[64,16384]{1,0:T(8,128)S(1)} %get-tuple-element.134.kept, f32[64,16384]{1,0:T(8,128)S(1)} %get-tuple-element.135.found), custom_call_target="tpu_custom_call" | custom-call | tf_op jit(solution)/shard_map/cond/branch_2_fun/write/pallas_call | solution.py:775
Async XLA Ops:
  0.6 2.9 %copy-start = (bf16[2,7,256,256]{3,2,1,0:T(8,128)(2,1)S(1)}, bf16[2,7,256,256]{3,2,1,0:T(8,128)(2,1)}, u32[]{:S(2)}) copy-start(bf16[2,7,256,256]{3,2,1,0:T(8,128)(2,1)} %blocks.1) | copy-start | bytes 5505028
  0.6 2.9 %copy-start.1 = (s32[64,7]{0,1:T(8,128)S(1)}, s32[64,7]{0,1:T(8,128)}, u32[]{:S(2)}) copy-start(s32[64,7]{0,1:T(8,128)} %param.18) | copy-start | bytes 5380
